TPU v7x, 32 devices: a whole 2x2x4 slice. The times are simulated.
32 devices in a mesh: groups: 2 (over y), row: 4 (over z), col: 4 (over x, core).
Axes of the slice: x: 2, y: 2, z: 4, core: 2. Of those that a mesh axis runs over, the one named last changes fastest.
Arguments:
- pair: bfloat16 [512, 256, 128], P(('groups', 'row'), 'col'), parts along dimension 0, may hold values from -300 to 300
- single: bfloat16 [512, 384], P(('groups', 'row')), parts along dimension 0, may hold values from -6 to 6
- token_mask: int32 [512], P(('groups', 'col')), parts along dimension 0, may hold values from 0 to 1, as said below
- pair_gain: float32 [128], replicated, may hold values from 0.25 to 1.75
- transition_in: bfloat16 [128, 1024], replicated, may hold values from -0.5 to 0.5
- transition_out: bfloat16 [512, 128], replicated, may hold values from -0.25 to 0.25
- bias_weight: float32 [128, 16], replicated, may hold values from -0.9 to 0.9
- bin_weight: float32 [128, 64], replicated, may hold values from -0.5 to 0.5
- single_gain: float32 [384], replicated, may hold values from 0.25 to 1.75
- attention_in: bfloat16 [384, 1536], replicated, may hold values from -0.3125 to 0.3125
- attention_out: bfloat16 [384, 384], replicated, may hold values from -0.8984375 to 0.8984375
Outputs:
- distogram: float32 [512, 256, 64], P(('groups', 'row'), 'col'), parts along dimension 0
- single_update: bfloat16 [512, 384], P(('groups', 'row')), parts along dimension 0
There are 2 independent parts, one for each index of `groups`. A program takes and returns all parts, laid end to end along the dimension named above; an argument that names none is the same for every part. Nothing has to cross between parts.
Inputs may be any that keep to these rules, and one draw needn't show every extreme that they name: `token_mask`: 1 on a prefix of at least 128 tokens, 0 after it; at least the last token is 0.
All inputs are finite; a program needn't handle non-finite values.
Results may differ from a plain program's by a relative error of at most 0.014.
Values may be sent and summed in bfloat16 or wider, within the bound.
A program may use at most 64 MiB of HBM per device.

v0:
```python
import functools
import math

import jax
import jax.numpy as jnp
from jax import lax
from jax.experimental import pallas as pl
from jax.experimental.pallas import tpu as pltpu
from jax.sharding import PartitionSpec as P

MESH = pl.DeviceIdType.MESH
F32 = jnp.float32
BF16 = jnp.bfloat16


def dot(a, b):
    return jnp.dot(a, b, preferred_element_type=F32)


def layer_norm(values, gain):
    average = jnp.mean(values, axis=-1, keepdims=True)
    centered = values - average
    variance = jnp.mean(centered * centered, axis=-1, keepdims=True)
    return centered * lax.rsqrt(variance + 1e-05) * gain


def split(value):
    high = value.astype(BF16)
    return high, (value - high.astype(F32)).astype(BF16)


def kernel(
    side, chunks,
    pair_hbm, single_hbm, *rest,
):
    far = rest[:8]
    result, gated_out = rest[8:10]
    pair, single, *near = rest[10:20]
    mask, pair_gain, transition_in, transition_out, bias_t, bin_t, single_gain, attention_in = near
    pair_sem, load_sem = rest[20:22]
    (
        own, packed, mirrored, relay, key_rows, parts, weights, queries, gates, keys, vals,
        spread, gather,
        key_send, key_recv, send_sem, recv_sem, relay_recv, relay_send, part_send, part_recv,
        back_out, back_in, back_send, back_recv,
    ) = rest[22:]
    g, r, c = (lax.axis_index(name) for name in ("groups", "row", "col"))
    off = r != c
    diagonal = r == c
    tile_rows, width = single.shape
    tile_cols = key_rows.shape[0]
    heads = bias_t.shape[0]
    bins = bin_t.shape[0]
    head_width = width // heads
    hidden = transition_out.shape[0]
    lanes = pair.shape[1]
    half = tile_rows * tile_cols // 2
    n = half // chunks
    block = n // tile_cols
    quarter = tile_rows // 4
    unit = half // 2 // chunks
    relayed = [u for u in range(chunks) if u % 4 != 3]
    above = r < c
    below = r > c

    def first_row(q):
        return block * q + quarter * (2 * q // chunks)

    def load(q, side_half):
        start = (first_row(q) + side_half * quarter) * tile_cols
        rows = pl.ds(pl.multiple_of(start, n), n)
        return pltpu.make_async_copy(pair_hbm.at[rows], pair.at[rows], pair_sem.at[side_half, q])

    loads = [
        pltpu.make_async_copy(source, target, load_sem.at[index])
        for index, (source, target) in enumerate(zip((single_hbm, *far), (single, *near)))
    ]
    for index in (0, 5, 6, 2, 3, 4):
        loads[index].start()
    for q in range(chunks):
        load(q, 0).start()
        load(q, 1).start()
    for index in (1, 7, 8):
        loads[index].start()

    barrier = pltpu.get_barrier_semaphore()
    for step in range(1, side):
        pl.semaphore_signal(barrier, inc=1, device_id=(g, r, lax.rem(c + step, side)), device_id_type=MESH)
        pl.semaphore_signal(barrier, inc=1, device_id=(g, lax.rem(r + step, side), c), device_id_type=MESH)

    @pl.when(off)
    def _():
        pl.semaphore_signal(barrier, inc=1, device_id=(g, c, r), device_id_type=MESH)

    loads[5].wait()
    loads[6].wait()
    stacked = jnp.concatenate(
        [bin_t[...], bias_t[...], jnp.zeros((lanes - heads - bins, lanes), F32)], axis=0
    ).T
    high, low = split(stacked)
    weights[0:lanes, 0:lanes] = high
    weights[lanes:, 0:lanes] = high
    weights[0:lanes, lanes:] = low
    weights[lanes:, lanes:] = low
    feature = lax.broadcasted_iota(jnp.int32, (width, lanes), 0)
    head = lax.broadcasted_iota(jnp.int32, (width, lanes), 1) - bins
    gather[...] = jnp.where(
        (feature >= head * head_width) & (feature < (head + 1) * head_width), 1.0, 0.0
    ).astype(BF16)
    feature = lax.broadcasted_iota(jnp.int32, (lanes, width), 1)
    head = lax.broadcasted_iota(jnp.int32, (lanes, width), 0) - bins
    spread[...] = jnp.where(
        (feature >= head * head_width) & (feature < (head + 1) * head_width), 1.0, 0.0
    ).astype(BF16)

    @pl.when(off)
    def _():
        pl.semaphore_wait(barrier, 2 * (side - 1) + 1)

    @pl.when(diagonal)
    def _():
        pl.semaphore_wait(barrier, 2 * (side - 1))

    key_copy = pltpu.make_async_remote_copy(
        src_ref=single, dst_ref=key_rows, send_sem=key_send, recv_sem=key_recv,
        device_id=(g, c, r), device_id_type=MESH,
    )

    loads[0].wait()

    def part(u):
        return pl.ds(pl.multiple_of(u * unit, unit), unit)

    def direct(u):
        return pltpu.make_async_remote_copy(
            src_ref=packed.at[part(u)], dst_ref=mirrored.at[part(u)],
            send_sem=send_sem.at[u], recv_sem=recv_sem.at[u],
            device_id=(g, c, r), device_id_type=MESH,
        )

    def to_relay(u):
        t = u - u // 4
        return pltpu.make_async_remote_copy(
            src_ref=packed.at[part(u)], dst_ref=relay.at[c, part(t)],
            send_sem=send_sem.at[u], recv_sem=relay_recv.at[c, t],
            device_id=(g, r, r), device_id_type=MESH,
        )

    def forward(k, t):
        u = relayed[t]
        return pltpu.make_async_remote_copy(
            src_ref=relay.at[k, part(t)], dst_ref=mirrored.at[part(u)],
            send_sem=relay_send.at[k, t], recv_sem=recv_sem.at[u],
            device_id=(g, k, r), device_id_type=MESH,
        )

    def arrived(k, t):
        return pltpu.make_async_remote_copy(
            src_ref=relay.at[k, part(t)], dst_ref=relay.at[k, part(t)],
            send_sem=relay_send.at[k, t], recv_sem=relay_recv.at[k, t],
            device_id=(g, k, r), device_id_type=MESH,
        )

    def back(u):
        return pltpu.make_async_remote_copy(
            src_ref=back_out.at[part(u)], dst_ref=back_in.at[part(u)],
            send_sem=back_send.at[u], recv_sem=back_recv.at[u],
            device_id=(g, c, r), device_id_type=MESH,
        )

    def forward_all(t):
        for step in range(1, side):
            k = lax.rem(r + step, side)
            arrived(k, t).wait_recv()
            forward(k, t).start()

    def send(u):
        @pl.when(lax.rem(u, 4) != 3)
        def _():
            to_relay(u).start()

        @pl.when(lax.rem(u, 4) == 3)
        def _():
            direct(u).start()

    @pl.when(off)
    def _():
        key_copy.start()

    @pl.when(diagonal)
    def _():
        key_rows[...] = single[...]

    for index in (2, 3, 4):
        loads[index].wait()

    def transition(q, carry):
        lower = pl.ds(pl.multiple_of(first_row(q) * tile_cols, n), n)
        upper = pl.ds(pl.multiple_of((first_row(q) + quarter) * tile_cols, n), n)
        load(q, 0).wait()
        load(q, 1).wait()
        flat = jnp.concatenate([pair[lower], pair[upper]], axis=0).astype(F32)
        normed = layer_norm(flat, pair_gain[...]).astype(BF16)
        total = flat
        wide = min(256, hidden)
        for start in range(0, hidden, wide):
            gate = 0.5 * dot(normed, transition_in[:, start : start + wide])
            up = dot(normed, transition_in[:, hidden + start : hidden + start + wide])
            inner = ((gate + gate * jnp.tanh(gate)) * up).astype(BF16)
            total = total + dot(inner, transition_out[start : start + wide])
        product = dot(jnp.concatenate(split(total), axis=1), weights[...])
        product = product[:, :lanes] + product[:, lanes:]
        own[lower] = product[:n]
        own[upper] = product[n:]

        @pl.when(above)
        def _():
            blocks = product.reshape(2 * block, tile_cols, lanes)
            start = tile_cols // 2
            low = blocks[:, start : start + quarter].reshape(unit, lanes)
            high = blocks[:, start + quarter :].reshape(unit, lanes)
            lane = lax.broadcasted_iota(jnp.int32, (unit, lanes), 1)
            packed[part(q)] = jnp.where(lane < bins, low, pltpu.roll(high, bins, 1))
            send(q)

        @pl.when(below & (q < chunks // 2))
        def _():
            lane = lax.broadcasted_iota(jnp.int32, (n, lanes), 1)
            rows = pl.ds(pl.multiple_of(q * n, n), n)
            packed[rows] = jnp.where(lane < bins, product[:n], pltpu.roll(product[n:], bins, 1))
            send(2 * q)
            send(2 * q + 1)

        for t, u in enumerate(relayed):
            if u + 2 < chunks:
                @pl.when(diagonal & (q == u + 2))
                def _(t=t):
                    forward_all(t)

        return carry

    lax.fori_loop(0, chunks, transition, 0)

    lane = lax.broadcasted_iota(jnp.int32, (unit, lanes), 1)
    lower_lanes = lane < bins

    def soft(logits):
        lower = lower_lanes[: logits.shape[0]]

        def halves(join, value, empty):
            return jnp.where(
                lower,
                join(jnp.where(lower, value, empty), axis=-1, keepdims=True),
                join(jnp.where(lower, empty, value), axis=-1, keepdims=True),
            )

        raised = jnp.exp(logits - halves(jnp.max, logits, -jnp.inf))
        return raised / halves(jnp.sum, raised, 0.0)

    def place_of(u, s):
        return first_row(u) + s + (quarter - block) * (s // block)

    def joined(near, far):
        return jnp.where(lower_lanes[: near.shape[0]], near, pltpu.roll(far, bins, 1))

    def apart(value, near, far):
        lower = lower_lanes[: value.shape[0]]
        return jnp.where(lower, value, near), jnp.where(lower, pltpu.roll(value, bins, 1), far)

    columns = unit // tile_rows

    def own_views(u):
        views = []
        if_above = [
            tuple(pl.ds(columns * u + s + quarter * h, tile_rows, stride=tile_cols) for h in range(2))
            for s in range(columns)
        ]
        if_below = [
            tuple(
                pl.ds((2 + h) * quarter * tile_cols + place_of(u, s), quarter, stride=tile_cols)
                for h in range(2)
            )
            for s in range(2 * block)
        ]
        return if_above, if_below

    def finish(u, carry):
        def settle(views):
            nears = [own[near, :] for near, _ in views]
            fars = [own[far, :] for _, far in views]
            near, far = jnp.concatenate(nears, axis=0), jnp.concatenate(fars, axis=0)
            value = soft(joined(near, far) + mirrored[part(u)])
            back_out[part(u)] = value.astype(BF16)
            back(u).start()
            near, far = apart(value, near, far)
            size = unit // len(views)
            for s, (near_view, far_view) in enumerate(views):
                own[near_view, :] = near[s * size : (s + 1) * size]
                own[far_view, :] = far[s * size : (s + 1) * size]

        @pl.when(off)
        def _():
            direct(u).wait_recv()

        if_above, if_below = own_views(u)

        @pl.when(above)
        def _():
            settle(if_above)

        @pl.when(below)
        def _():
            settle(if_below)

        return carry

    def collect(u, carry):
        back(u).wait_recv()
        value = back_in[part(u)].astype(F32)
        other = pltpu.roll(value, bins, 1)

        @pl.when(above)
        def _():
            for s in range(2 * block):
                start = place_of(u, s) * tile_cols + tile_cols // 2
                one = slice(s * quarter, (s + 1) * quarter)
                own[pl.ds(pl.multiple_of(start, quarter), quarter)] = value[one]
                own[pl.ds(pl.multiple_of(start + quarter, quarter), quarter)] = other[one]

        @pl.when(below)
        def _():
            start = pl.multiple_of(u * unit, unit)
            own[pl.ds(start, unit)] = value
            own[pl.ds(pl.multiple_of(start + quarter * tile_cols, unit), unit)] = other

        return carry

    def mirror_self(j, carry):
        def rows(start):
            return own[pl.ds(pl.multiple_of(start * tile_cols, tile_cols), tile_cols), :]

        def column(start):
            return own[pl.ds(start, tile_rows, stride=tile_cols), :]

        far = j + tile_cols // 2
        logits = joined(column(j), column(far)) + joined(rows(j), rows(far))
        result[pl.ds(j, tile_rows, stride=tile_cols // 2), :] = soft(logits)
        return carry

    def pack(t, carry):
        rows = group * tile_cols
        value = own[pl.ds(pl.multiple_of(t * rows, rows), rows)].reshape(group, tile_cols, lanes)
        low = value[:, : tile_cols // 2].reshape(rows // 2, lanes)
        high = value[:, tile_cols // 2 :].reshape(rows // 2, lanes)
        lane = lax.broadcasted_iota(jnp.int32, low.shape, 1)
        result[pl.ds(pl.multiple_of(t * rows // 2, rows // 2), rows // 2)] = jnp.where(
            lane < bins, low, pltpu.roll(high, bins, 1)
        )
        return carry

    @pl.when(diagonal)
    def _():
        for t, u in enumerate(relayed):
            if u + 2 >= chunks:
                forward_all(t)

    @pl.when(off)
    def _():
        lax.fori_loop(0, chunks // 2, finish, 0)

    for index in (1, 7, 8):
        loads[index].wait()
    single_scale = single_gain[...].reshape(1, width)
    query_normed = layer_norm(single[...].astype(F32), single_scale).astype(BF16)
    queries[...] = dot(query_normed, attention_in[:, :width]) * (1.0 / math.sqrt(head_width))
    gates[...] = dot(query_normed, attention_in[:, 3 * width :])

    @pl.when(off)
    def _():
        key_copy.wait()

    key_normed = layer_norm(key_rows[...].astype(F32), single_scale).astype(BF16)
    keys[...] = dot(key_normed, attention_in[:, width : 2 * width])
    vals[...] = dot(key_normed, attention_in[:, 2 * width : 3 * width])
    group = 8
    square = (tile_cols, tile_cols)
    same = lax.broadcasted_iota(jnp.int32, square, 0) == lax.broadcasted_iota(jnp.int32, square, 1)
    real_key = jnp.max(jnp.where(same, mask[...], 0), axis=1, keepdims=True) > 0
    lane = lax.broadcasted_iota(jnp.int32, (tile_cols, lanes), 1)
    kept = real_key & (lane >= bins) & (lane < bins + heads)

    def attend(t, carry):
        some = pl.ds(pl.multiple_of(t * group, group), group)
        rows = pl.ds(pl.multiple_of(t * group * tile_cols, group * tile_cols), group * tile_cols)
        product = queries[some][:, None, :] * keys[...][None]
        product = product.reshape(group * tile_cols, width).astype(BF16)
        scores = (dot(product, gather[...]) + own[rows]).reshape(group, tile_cols, lanes)
        scores = jnp.where(kept[None], scores, -1000000000.0)
        top = jnp.max(scores, axis=1)
        raised = jnp.exp(scores - top[:, None, :])
        total = jnp.sum(raised, axis=1)
        wide = dot(raised.reshape(group * tile_cols, lanes).astype(BF16), spread[...])
        summed = jnp.sum(wide.reshape(group, tile_cols, width) * vals[...][None], axis=1)
        lane = lax.broadcasted_iota(jnp.int32, (group, lanes), 1)
        parts[c, some, 0:lanes] = jnp.where(lane < bins, pltpu.roll(total, lanes - bins, 1), top)
        parts[c, some, lanes:] = summed
        return carry

    lax.fori_loop(0, tile_rows // group, attend, 0)

    def part_copy(source, target):
        return pltpu.make_async_remote_copy(
            src_ref=parts.at[source], dst_ref=parts.at[source],
            send_sem=part_send.at[target], recv_sem=part_recv.at[source],
            device_id=(g, r, target), device_id_type=MESH,
        )

    for step in range(1, side):
        part_copy(c, lax.rem(c + step, side)).start()

    @pl.when(off)
    def _():
        lax.fori_loop(chunks // 2, chunks, finish, 0)

    @pl.when(diagonal)
    def _():
        lax.fori_loop(0, tile_cols // 2, mirror_self, 0)

    for step in range(1, side):
        part_copy(lax.rem(c + step, side), lax.rem(c + step, side)).wait_recv()
    top = parts[0, :, 0:lanes]
    for k in range(1, side):
        top = jnp.maximum(top, parts[k, :, 0:lanes])
    factors = []
    total = jnp.zeros((tile_rows, lanes), F32)
    for k in range(side):
        stats = parts[k, :, 0:lanes]
        factor = jnp.exp(stats - top)
        total = total + factor * pltpu.roll(stats, bins, 1)
        factors.append(factor)
    lane = lax.broadcasted_iota(jnp.int32, (tile_rows, lanes), 1)
    real = (lane >= bins) & (lane < bins + heads)
    inverse = 1.0 / jnp.where(real, total, 1.0)
    attended = jnp.zeros((tile_rows, width), F32)
    for k in range(side):
        high, low = split(jnp.where(real, factors[k] * inverse, 0.0))
        attended = attended + (dot(high, spread[...]) + dot(low, spread[...])) * parts[k, :, lanes:]
    gated_out[...] = (jax.nn.sigmoid(gates[...]) * attended).astype(BF16)

    @pl.when(off)
    def _():
        lax.fori_loop(0, chunks, collect, 0)
        lax.fori_loop(0, tile_rows // group, pack, 0)

    for step in range(1, side):
        part_copy(c, lax.rem(c + step, side)).wait_send()

    @pl.when(off)
    def _():
        for q in range(chunks):
            direct(q).wait_send()
            back(q).wait_send()

    @pl.when(diagonal)
    def _():
        for t in range(len(relayed)):
            for step in range(1, side):
                forward(lax.rem(r + step, side), t).wait_send()


def unpack(packed, gated, attention_out, dist, update):
    count, tile_cols, bins = dist.shape
    value = packed[...].reshape(count, tile_cols // 2, 2 * bins)
    dist[:, : tile_cols // 2] = value[:, :, :bins]
    dist[:, tile_cols // 2 :] = value[:, :, bins:]

    @pl.when(pl.program_id(0) == 0)
    def _():
        update[...] = dot(gated[...], attention_out[...]).astype(BF16)


def body(
    side, pair, single, token_mask, pair_gain, transition_in, transition_out, bias_weight,
    bin_weight, single_gain, attention_in, attention_out,
):
    tile_rows, tile_cols, channels = pair.shape
    width = single.shape[1]
    bins = bin_weight.shape[1]
    rows = tile_rows * tile_cols
    chunks = 8
    unit = rows // 4 // chunks
    whole = pl.BlockSpec(memory_space=pltpu.VMEM)
    dma = pltpu.SemaphoreType.DMA
    operands = (
        pair.reshape(rows, channels), single, token_mask.reshape(1, tile_cols),
        pair_gain.reshape(1, -1), transition_in, transition_out, bias_weight.T, bin_weight.T,
        single_gain, attention_in,
    )
    probabilities, gated = pl.pallas_call(
        functools.partial(kernel, side, chunks),
        out_shape=(
            jax.ShapeDtypeStruct((rows // 2, channels), F32),
            jax.ShapeDtypeStruct((tile_rows, width), BF16),
        ),
        in_specs=[pl.BlockSpec(memory_space=pltpu.HBM)] * 10,
        out_specs=(whole, whole),
        scratch_shapes=[
            *[pltpu.VMEM(operand.shape, operand.dtype) for operand in operands],
            dma((2, chunks)), dma((len(operands) - 1,)),
            pltpu.VMEM((rows, channels), F32),
            pltpu.VMEM((rows // 4, channels), F32),
            pltpu.VMEM((rows // 4, channels), F32),
            pltpu.VMEM((side, chunks // 4 * 3 * unit, channels), F32),
            pltpu.VMEM((tile_cols, width), BF16),
            pltpu.VMEM((side, tile_rows, channels + width), F32),
            pltpu.VMEM((2 * channels, 2 * channels), BF16),
            pltpu.VMEM((tile_rows, width), F32),
            pltpu.VMEM((tile_rows, width), F32),
            pltpu.VMEM((tile_cols, width), F32),
            pltpu.VMEM((tile_cols, width), F32),
            pltpu.VMEM((channels, width), BF16),
            pltpu.VMEM((width, channels), BF16),
            dma, dma, dma((chunks,)), dma((chunks,)),
            dma((side, chunks // 4 * 3)), dma((side, chunks // 4 * 3)), dma((side,)), dma((side,)),
            pltpu.VMEM((rows // 4, channels), BF16), pltpu.VMEM((rows // 4, channels), BF16),
            dma((chunks,)), dma((chunks,)),
        ],
        compiler_params=pltpu.CompilerParams(
            collective_id=0, has_side_effects=True, vmem_limit_bytes=57 << 20
        ),
    )(*operands)
    steps = 2
    some = tile_rows // steps
    return pl.pallas_call(
        unpack,
        grid=(steps,),
        out_shape=(
            jax.ShapeDtypeStruct((tile_rows, tile_cols, bins), F32),
            jax.ShapeDtypeStruct((tile_rows, width), BF16),
        ),
        in_specs=[
            pl.BlockSpec((some * tile_cols // 2, channels), lambda i: (i, 0)),
            pl.BlockSpec((tile_rows, width), lambda i: (0, 0)),
            pl.BlockSpec((width, width), lambda i: (0, 0)),
        ],
        out_specs=(
            pl.BlockSpec((some, tile_cols, bins), lambda i: (i, 0, 0)),
            pl.BlockSpec((tile_rows, width), lambda i: (0, 0)),
        ),
        compiler_params=pltpu.CompilerParams(vmem_limit_bytes=57 << 20),
    )(probabilities, gated, attention_out)


def solution(mesh):
    in_specs = (
        P(("groups", "row"), "col", None),
        P(("groups", "row"), None),
        P(("groups", "col")),
        P(), P(), P(), P(), P(), P(), P(), P(),
    )
    out_specs = (P(("groups", "row"), "col", None), P(("groups", "row"), None))
    return jax.shard_map(
        functools.partial(body, mesh.shape["row"]),
        mesh=mesh, in_specs=in_specs, out_specs=out_specs, check_vma=False,
    )
```

profile of v0, /device:TPU:0, one launch (start us, length us, event | category | flops | bytes accessed | tf_op | source)
XLA Modules:
  0.0 38.9 jit_solution(17480397804895063879)
XLA Ops:
  0.6 35.4 %shard_map.122 = (f32[2048,128]{1,0:T(8,128)}, bf16[64,384]{1,0:T(8,128)(2,1)}) custom-call(bf16[4096,128]{1,0:T(8,128)(2,1)} %bitcast.5, bf16[64,384]{1,0:T(8,128)(2,1)} %single_hbm.1, s32[1,64]{1,0:T(1,128)} %bitcast.8, f32[1,128]{1,0:T(1,128)} %bitcast.9, bf16[128,1024]{1,0:T(8,128)(2,1)} %rest_2_.1, bf16[512,128]{1,0:T(8,128)(2,1)} %rest_3_.1, ...), custom_call_target="tpu_custom_call" | custom-call | tf_op jit(solution)/shard_map/pallas_call | solution.py:499
  36.1 2.8 %shard_map.123 = (f32[64,64,64]{2,1,0:T(8,128)}, bf16[64,384]{1,0:T(8,128)(2,1)}) custom-call(f32[2048,128]{1,0:T(8,128)} %get-tuple-element.4.packed, bf16[64,384]{1,0:T(8,128)(2,1)} %get-tuple-element.5.gated, bf16[384,384]{1,0:T(8,128)(2,1)} %attention_out.1), custom_call_target="tpu_custom_call" | custom-call | tf_op jit(solution)/shard_map/pallas_call | solution.py:534
where the time goes:
time: 39 us; the launch traced here: 38.9 us
  Pallas kernels  38.2 us (98%)
  between operations  0.64 us (2%)
    pallas_call x1, Pallas kernels, body(): pl.pallas_call(functools.partial(kernel, side, chunks), out_shape=(jax.Sh...  35.4 us
    pallas_call x1, Pallas kernels, body(): pl.pallas_call(unpack, grid=(steps,), out_shape=(jax.ShapeDtypeStruct((ti...  2.83 us

commit v1 on v0

v1 whole, which is shorter than its diff:
```python
import functools
import math

import jax
import jax.numpy as jnp
from jax import lax
from jax.experimental import pallas as pl
from jax.experimental.pallas import tpu as pltpu
from jax.sharding import PartitionSpec as P

MESH = pl.DeviceIdType.MESH
F32 = jnp.float32
BF16 = jnp.bfloat16
LAG = 3


def dot(a, b):
    return jnp.dot(a, b, preferred_element_type=F32)


def layer_norm(values, gain):
    average = jnp.mean(values, axis=-1, keepdims=True)
    centered = values - average
    variance = jnp.mean(centered * centered, axis=-1, keepdims=True)
    return centered * lax.rsqrt(variance + 1e-05) * gain


def split(value):
    high = value.astype(BF16)
    return high, (value - high.astype(F32)).astype(BF16)


def kernel(
    side, chunks, relayed,
    pair_hbm, single_hbm, *rest,
):
    far = rest[:8]
    result, gated_out = rest[8:10]
    pair, single, *near = rest[10:20]
    mask, pair_gain, transition_in, transition_out, bias_t, bin_t, single_gain, attention_in = near
    pair_sem, load_sem = rest[20:22]
    (
        own, packed, mirrored, relay, key_rows, parts, first, second, normed, inner,
        queries, gates, keys, vals, spread, gather,
        key_send, key_recv, send_sem, recv_sem, relay_recv, relay_send, part_send, part_recv,
    ) = rest[22:]
    g, r, c = (lax.axis_index(name) for name in ("groups", "row", "col"))
    off = r != c
    diagonal = r == c
    tile_rows, width = single.shape
    tile_cols = key_rows.shape[0]
    heads = bias_t.shape[0]
    bins = bin_t.shape[0]
    head_width = width // heads
    hidden = transition_out.shape[0]
    lanes = pair.shape[1]
    half = tile_rows * tile_cols // 2
    n = half // chunks
    block = n // tile_cols

    def part(q):
        return pl.ds(pl.multiple_of(q * n, n), n)

    def upper(q):
        return pl.ds(pl.multiple_of(half + q * n, n), n)

    def load(q, side_half):
        rows = upper(q) if side_half else part(q)
        return pltpu.make_async_copy(pair_hbm.at[rows], pair.at[rows], pair_sem.at[side_half, q])

    loads = [
        pltpu.make_async_copy(source, target, load_sem.at[index])
        for index, (source, target) in enumerate(zip((single_hbm, *far), (single, *near)))
    ]
    for index in (0, 5, 6, 4, 2, 3):
        loads[index].start()
    for q in range(chunks):
        load(q, 0).start()
        load(q, 1).start()
    for index in (1, 7, 8):
        loads[index].start()

    barrier = pltpu.get_barrier_semaphore()
    for step in range(1, side):
        pl.semaphore_signal(barrier, inc=1, device_id=(g, r, lax.rem(c + step, side)), device_id_type=MESH)
        pl.semaphore_signal(barrier, inc=1, device_id=(g, lax.rem(r + step, side), c), device_id_type=MESH)

    @pl.when(off)
    def _():
        pl.semaphore_signal(barrier, inc=1, device_id=(g, c, r), device_id_type=MESH)

    loads[5].wait()
    loads[6].wait()
    stacked = jnp.concatenate(
        [bin_t[...], bias_t[...], jnp.zeros((lanes - heads - bins, lanes), F32)], axis=0
    ).T
    high, low = split(stacked)
    loads[4].wait()
    second[hidden:, :lanes] = high
    second[hidden:, lanes:] = low
    joint = dot(transition_out[...], second[hidden:])
    high, low = split(joint[:, :lanes] + joint[:, lanes:])
    second[:hidden, :lanes] = high
    second[:hidden, lanes:] = low
    feature = lax.broadcasted_iota(jnp.int32, (width, lanes), 0)
    head = lax.broadcasted_iota(jnp.int32, (width, lanes), 1) - bins
    gather[...] = jnp.where(
        (feature >= head * head_width) & (feature < (head + 1) * head_width), 1.0, 0.0
    ).astype(BF16)
    feature = lax.broadcasted_iota(jnp.int32, (lanes, width), 1)
    head = lax.broadcasted_iota(jnp.int32, (lanes, width), 0) - bins
    spread[...] = jnp.where(
        (feature >= head * head_width) & (feature < (head + 1) * head_width), 1.0, 0.0
    ).astype(BF16)

    @pl.when(off)
    def _():
        pl.semaphore_wait(barrier, 2 * (side - 1) + 1)

    @pl.when(diagonal)
    def _():
        pl.semaphore_wait(barrier, 2 * (side - 1))

    key_copy = pltpu.make_async_remote_copy(
        src_ref=single, dst_ref=key_rows, send_sem=key_send, recv_sem=key_recv,
        device_id=(g, c, r), device_id_type=MESH,
    )

    loads[0].wait()

    def direct(u):
        return pltpu.make_async_remote_copy(
            src_ref=packed.at[part(u)], dst_ref=mirrored.at[part(u)],
            send_sem=send_sem.at[u], recv_sem=recv_sem.at[u],
            device_id=(g, c, r), device_id_type=MESH,
        )

    def to_relay(t):
        u = relayed[t]
        return pltpu.make_async_remote_copy(
            src_ref=packed.at[part(u)], dst_ref=relay.at[c, part(t)],
            send_sem=send_sem.at[u], recv_sem=relay_recv.at[c, t],
            device_id=(g, r, r), device_id_type=MESH,
        )

    def forward(k, t):
        return pltpu.make_async_remote_copy(
            src_ref=relay.at[k, part(t)], dst_ref=mirrored.at[part(relayed[t])],
            send_sem=relay_send.at[k, t], recv_sem=recv_sem.at[relayed[t]],
            device_id=(g, k, r), device_id_type=MESH,
        )

    def arrived(k, t):
        return pltpu.make_async_remote_copy(
            src_ref=relay.at[k, part(t)], dst_ref=relay.at[k, part(t)],
            send_sem=relay_send.at[k, t], recv_sem=relay_recv.at[k, t],
            device_id=(g, k, r), device_id_type=MESH,
        )

    def forward_all(t):
        for step in range(1, side):
            k = lax.rem(r + step, side)
            arrived(k, t).wait_recv()
            forward(k, t).start()

    @pl.when(off)
    def _():
        key_copy.start()

    @pl.when(diagonal)
    def _():
        key_rows[...] = single[...]

    loads[2].wait()
    loads[3].wait()
    first[:, :hidden] = transition_in[:, :hidden] * jnp.asarray(0.5, BF16)
    first[:, hidden:] = transition_in[:, hidden:]
    wide = min(256, hidden)

    def slot(q):
        return pl.ds(pl.multiple_of(lax.rem(q, 2) * 2 * n, 2 * n), 2 * n)

    def tokens(q):
        return jnp.concatenate([pair[part(q)], pair[upper(q)]], axis=0)

    def norm(q):
        normed[slot(q)] = layer_norm(tokens(q).astype(F32), pair_gain[...]).astype(BF16)

    def expand(q):
        some = normed[slot(q)]
        for start in range(0, hidden, wide):
            gate = dot(some, first[:, start : start + wide])
            up = dot(some, first[:, hidden + start : hidden + start + wide])
            inner[slot(q), start : start + wide] = ((gate + gate * jnp.tanh(gate)) * up).astype(BF16)

    def project(q):
        both = dot(jnp.concatenate([inner[slot(q)], tokens(q)], axis=1), second[...])
        product = both[:, :lanes] + both[:, lanes:]
        own[part(q)] = product[:n]
        own[upper(q)] = product[n:]
        lane = lax.broadcasted_iota(jnp.int32, (n, lanes), 1)
        logits = 0.25 * jnp.where(lane < bins, product[:n], pltpu.roll(product[n:], bins, 1))
        square = logits * logits
        packed[part(q)] = (square * square * logits).astype(BF16)

    def ready(q):
        load(q, 0).wait()
        load(q, 1).wait()

    def send(q):
        for u in range(chunks):
            if u in relayed:
                @pl.when(off & (q == u))
                def _(u=u):
                    to_relay(relayed.index(u)).start()

            else:
                @pl.when(off & (q == u))
                def _(u=u):
                    direct(u).start()

        @pl.when(diagonal)
        def _():
            mirrored[part(q)] = packed[part(q)]

        for t, u in enumerate(relayed):
            if u + LAG < chunks:
                @pl.when(diagonal & (q == u + LAG))
                def _(t=t):
                    forward_all(t)

    ready(0)
    norm(0)
    ready(1)
    norm(1)
    expand(0)

    def transition(q, carry):
        ready(q + 2)
        project(q)
        expand(q + 1)
        norm(q + 2)
        send(q)
        return carry

    lax.fori_loop(0, chunks - 2, transition, 0)
    project(chunks - 2)
    expand(chunks - 1)
    send(chunks - 2)
    project(chunks - 1)
    send(chunks - 1)

    @pl.when(diagonal)
    def _():
        for t, u in enumerate(relayed):
            if u + LAG >= chunks:
                forward_all(t)

    for index in (1, 7, 8):
        loads[index].wait()
    single_scale = single_gain[...].reshape(1, width)
    query_normed = layer_norm(single[...].astype(F32), single_scale).astype(BF16)
    queries[...] = dot(query_normed, attention_in[:, :width]) * (1.0 / math.sqrt(head_width))
    gates[...] = dot(query_normed, attention_in[:, 3 * width :])

    @pl.when(off)
    def _():
        key_copy.wait()

    key_normed = layer_norm(key_rows[...].astype(F32), single_scale).astype(BF16)
    keys[...] = dot(key_normed, attention_in[:, width : 2 * width])
    vals[...] = dot(key_normed, attention_in[:, 2 * width : 3 * width])
    group = 8
    square = (tile_cols, tile_cols)
    same = lax.broadcasted_iota(jnp.int32, square, 0) == lax.broadcasted_iota(jnp.int32, square, 1)
    real_key = jnp.max(jnp.where(same, mask[...], 0), axis=1, keepdims=True) > 0
    lane = lax.broadcasted_iota(jnp.int32, (tile_cols, lanes), 1)
    kept = real_key & (lane >= bins) & (lane < bins + heads)

    def attend(t, carry):
        some = pl.ds(pl.multiple_of(t * group, group), group)
        rows = pl.ds(pl.multiple_of(t * group * tile_cols, group * tile_cols), group * tile_cols)
        product = queries[some][:, None, :] * keys[...][None]
        product = product.reshape(group * tile_cols, width).astype(BF16)
        scores = (dot(product, gather[...]) + own[rows]).reshape(group, tile_cols, lanes)
        scores = jnp.where(kept[None], scores, -1000000000.0)
        top = jnp.max(scores, axis=1)
        raised = jnp.exp(scores - top[:, None, :])
        total = jnp.sum(raised, axis=1)
        wide = dot(raised.reshape(group * tile_cols, lanes).astype(BF16), spread[...])
        summed = jnp.sum(wide.reshape(group, tile_cols, width) * vals[...][None], axis=1)
        lane = lax.broadcasted_iota(jnp.int32, (group, lanes), 1)
        parts[c, some, 0:lanes] = jnp.where(lane < bins, pltpu.roll(total, lanes - bins, 1), top)
        parts[c, some, lanes:] = summed
        return carry

    lax.fori_loop(0, tile_rows // group, attend, 0)

    def part_copy(source, target):
        return pltpu.make_async_remote_copy(
            src_ref=parts.at[source], dst_ref=parts.at[source],
            send_sem=part_send.at[target], recv_sem=part_recv.at[source],
            device_id=(g, r, target), device_id_type=MESH,
        )

    for step in range(1, side):
        part_copy(c, lax.rem(c + step, side)).start()

    lane = lax.broadcasted_iota(jnp.int32, (tile_rows, lanes), 1)
    lower_lanes = lane < bins
    same_half = (lax.broadcasted_iota(jnp.int32, (lanes, lanes), 0) < bins) == (
        lax.broadcasted_iota(jnp.int32, (lanes, lanes), 1) < bins
    )
    adder = jnp.where(same_half, 1.0, 0.0).astype(BF16)

    def finish(u, carry):
        @pl.when(off)
        def _():
            direct(u).wait_recv()

        raised = []
        for s in range(block):
            j = u * block + s
            near = own[pl.ds(j, tile_rows, stride=tile_cols), :]
            far = own[pl.ds(j + tile_cols // 2, tile_rows, stride=tile_cols), :]
            coded = mirrored[pl.ds(pl.multiple_of(j * tile_rows, tile_rows), tile_rows)].astype(F32)
            size = jnp.exp2(jnp.log(jnp.abs(coded)) * (0.2 / math.log(2.0)) + 2.0)
            other = jnp.where(coded < 0, -size, size)
            logits = jnp.where(lower_lanes, near, pltpu.roll(far, bins, 1)) + other
            top = jnp.where(
                lower_lanes,
                jnp.max(jnp.where(lower_lanes, logits, -jnp.inf), axis=-1, keepdims=True),
                jnp.max(jnp.where(lower_lanes, -jnp.inf, logits), axis=-1, keepdims=True),
            )
            raised.append(jnp.exp(logits - top))
        value = jnp.concatenate(raised, axis=0)
        value = value / dot(value.astype(BF16), adder)
        for s in range(block):
            result[pl.ds(u * block + s, tile_rows, stride=tile_cols // 2), :] = value[
                s * tile_rows : (s + 1) * tile_rows
            ]
        return carry

    lax.fori_loop(0, chunks, finish, 0)

    for step in range(1, side):
        part_copy(lax.rem(c + step, side), lax.rem(c + step, side)).wait_recv()
    top = parts[0, :, 0:lanes]
    for k in range(1, side):
        top = jnp.maximum(top, parts[k, :, 0:lanes])
    factors = []
    total = jnp.zeros((tile_rows, lanes), F32)
    for k in range(side):
        stats = parts[k, :, 0:lanes]
        factor = jnp.exp(stats - top)
        total = total + factor * pltpu.roll(stats, bins, 1)
        factors.append(factor)
    real = (lane >= bins) & (lane < bins + heads)
    inverse = 1.0 / jnp.where(real, total, 1.0)
    attended = jnp.zeros((tile_rows, width), F32)
    for k in range(side):
        high, low = split(jnp.where(real, factors[k] * inverse, 0.0))
        attended = attended + (dot(high, spread[...]) + dot(low, spread[...])) * parts[k, :, lanes:]
    gated_out[...] = (jax.nn.sigmoid(gates[...]) * attended).astype(BF16)

    for step in range(1, side):
        part_copy(c, lax.rem(c + step, side)).wait_send()

    @pl.when(off)
    def _():
        for q in range(chunks):
            direct(q).wait_send()

    @pl.when(diagonal)
    def _():
        for t in range(len(relayed)):
            for step in range(1, side):
                forward(lax.rem(r + step, side), t).wait_send()


def unpack(packed, gated, attention_out, dist, update):
    count, tile_cols, bins = dist.shape
    value = packed[...].reshape(count, tile_cols // 2, 2 * bins)
    dist[:, : tile_cols // 2] = value[:, :, :bins]
    dist[:, tile_cols // 2 :] = value[:, :, bins:]

    @pl.when(pl.program_id(0) == 0)
    def _():
        update[...] = dot(gated[...], attention_out[...]).astype(BF16)


def body(
    side, pair, single, token_mask, pair_gain, transition_in, transition_out, bias_weight,
    bin_weight, single_gain, attention_in, attention_out,
):
    tile_rows, tile_cols, channels = pair.shape
    width = single.shape[1]
    bins = bin_weight.shape[1]
    rows = tile_rows * tile_cols
    chunks = 8
    relayed = (0, 2, 4, 6)
    n = rows // 2 // chunks
    hidden = transition_out.shape[0]
    whole = pl.BlockSpec(memory_space=pltpu.VMEM)
    dma = pltpu.SemaphoreType.DMA
    operands = (
        pair.reshape(rows, channels), single, token_mask.reshape(1, tile_cols),
        pair_gain.reshape(1, -1), transition_in, transition_out, bias_weight.T, bin_weight.T,
        single_gain, attention_in,
    )
    probabilities, gated = pl.pallas_call(
        functools.partial(kernel, side, chunks, relayed),
        out_shape=(
            jax.ShapeDtypeStruct((rows // 2, channels), F32),
            jax.ShapeDtypeStruct((tile_rows, width), BF16),
        ),
        in_specs=[pl.BlockSpec(memory_space=pltpu.HBM)] * 10,
        out_specs=(whole, whole),
        scratch_shapes=[
            *[pltpu.VMEM(operand.shape, operand.dtype) for operand in operands],
            dma((2, chunks)), dma((len(operands) - 1,)),
            pltpu.VMEM((rows, channels), F32),
            pltpu.VMEM((rows // 2, channels), BF16),
            pltpu.VMEM((rows // 2, channels), BF16),
            pltpu.VMEM((side, len(relayed) * n, channels), BF16),
            pltpu.VMEM((tile_cols, width), BF16),
            pltpu.VMEM((side, tile_rows, channels + width), F32),
            pltpu.VMEM((channels, 2 * hidden), BF16),
            pltpu.VMEM((hidden + channels, 2 * channels), BF16),
            pltpu.VMEM((4 * n, channels), BF16),
            pltpu.VMEM((4 * n, hidden), BF16),
            pltpu.VMEM((tile_rows, width), F32),
            pltpu.VMEM((tile_rows, width), F32),
            pltpu.VMEM((tile_cols, width), F32),
            pltpu.VMEM((tile_cols, width), F32),
            pltpu.VMEM((channels, width), BF16),
            pltpu.VMEM((width, channels), BF16),
            dma, dma, dma((chunks,)), dma((chunks,)),
            dma((side, len(relayed))), dma((side, len(relayed))), dma((side,)), dma((side,)),
        ],
        compiler_params=pltpu.CompilerParams(
            collective_id=0, has_side_effects=True, vmem_limit_bytes=57 << 20
        ),
    )(*operands)
    steps = 2
    some = tile_rows // steps
    return pl.pallas_call(
        unpack,
        grid=(steps,),
        out_shape=(
            jax.ShapeDtypeStruct((tile_rows, tile_cols, bins), F32),
            jax.ShapeDtypeStruct((tile_rows, width), BF16),
        ),
        in_specs=[
            pl.BlockSpec((some * tile_cols // 2, channels), lambda i: (i, 0)),
            pl.BlockSpec((tile_rows, width), lambda i: (0, 0)),
            pl.BlockSpec((width, width), lambda i: (0, 0)),
        ],
        out_specs=(
            pl.BlockSpec((some, tile_cols, bins), lambda i: (i, 0, 0)),
            pl.BlockSpec((tile_rows, width), lambda i: (0, 0)),
        ),
        compiler_params=pltpu.CompilerParams(vmem_limit_bytes=57 << 20),
    )(probabilities, gated, attention_out)


def solution(mesh):
    in_specs = (
        P(("groups", "row"), "col", None),
        P(("groups", "row"), None),
        P(("groups", "col")),
        P(), P(), P(), P(), P(), P(), P(), P(),
    )
    out_specs = (P(("groups", "row"), "col", None), P(("groups", "row"), None))
    return jax.shard_map(
        functools.partial(body, mesh.shape["row"]),
        mesh=mesh, in_specs=in_specs, out_specs=out_specs, check_vma=False,
    )
```

time: 39 us -> 30.1 us (0.77)
  the two profiles are of different devices: /device:TPU:0 before, /device:TPU:1 now
where the time goes in v1:
time: 30.1 us; the launch traced here: 29.9 us
  Pallas kernels  29.3 us (97%)
  between operations  0.64 us (2%)
    pallas_call x1, Pallas kernels, body(): pl.pallas_call(functools.partial(kernel, side, chunks, relayed), out_shap...  26.4 us
    pallas_call x1, Pallas kernels, body(): pl.pallas_call(unpack, grid=(steps,), out_shape=(jax.ShapeDtypeStruct((ti...  2.82 us

profile of v1, /device:TPU:1, one launch (start us, length us, event | category | flops | bytes accessed | tf_op | source)
XLA Modules:
  0.0 29.9 jit_solution(16928771515458203792)
XLA Ops:
  0.6 26.4 %shard_map.122 = (f32[2048,128]{1,0:T(8,128)}, bf16[64,384]{1,0:T(8,128)(2,1)}) custom-call(bf16[4096,128]{1,0:T(8,128)(2,1)} %bitcast.5, bf16[64,384]{1,0:T(8,128)(2,1)} %single_hbm.1, s32[1,64]{1,0:T(1,128)} %bitcast.8, f32[1,128]{1,0:T(1,128)} %bitcast.9, bf16[128,1024]{1,0:T(8,128)(2,1)} %rest_2_.1, bf16[512,128]{1,0:T(8,128)(2,1)} %rest_3_.1, ...), custom_call_target="tpu_custom_call" | custom-call | tf_op jit(solution)/shard_map/pallas_call | solution.py:411
  27.1 2.8 %shard_map.123 = (f32[64,64,64]{2,1,0:T(8,128)}, bf16[64,384]{1,0:T(8,128)(2,1)}) custom-call(f32[2048,128]{1,0:T(8,128)} %get-tuple-element.4.packed, bf16[64,384]{1,0:T(8,128)(2,1)} %get-tuple-element.5.gated, bf16[384,384]{1,0:T(8,128)(2,1)} %attention_out.1), custom_call_target="tpu_custom_call" | custom-call | tf_op jit(solution)/shard_map/pallas_call | solution.py:447
